TPU v7x, 768 devices: a whole 4x8x12 slice. The times are simulated.
768 devices in a mesh: section: 32 (over y, x_lo, core), depth: 2 (over x_hi), res: 12 (over z).
Axes of the slice: x: 4 (x_hi: 2, x_lo: 2; x = x_hi * 2 + x_lo), y: 8, z: 12, core: 2. Of those that a mesh axis runs over, the one named last changes fastest.
Arguments:
- slab: bfloat16 [32, 48, 96, 768], P('section', ('depth', 'res')), may hold values from -6 to 6
- tokens: int32 [48, 96], P(('depth', 'res')), may hold values from 0 to 32
- lengths: int32 [32, 48], P('section'), may hold values from 24 to 96, as said below
- embed: bfloat16 [33, 768], replicated, may hold values from -6 to 6
- row_qkv: bfloat16 [32, 768, 2304], P('section'), may hold values from -1 to 1
- row_out: bfloat16 [32, 768, 768], P('section'), may hold values from -0.21875 to 0.21875
- col_qkv: bfloat16 [32, 768, 2304], P('section'), may hold values from -1 to 1
- col_out: bfloat16 [32, 768, 768], P('section'), may hold values from -0.21875 to 0.21875
Outputs:
- next_slab: bfloat16 [32, 48, 96, 768], P('section', ('depth', 'res'))
Inputs may be any that keep to these rules, and one draw needn't show every extreme that they name: `lengths`: row 0 of every section's micro-batch has length 96.
All inputs are finite; a program needn't handle non-finite values.
Results may differ from a plain program's by a relative error of at most 0.012.
Values may be sent and summed in bfloat16 or wider, within the bound.
No kernel may reach another device: no remote copies, remote signals or barrier semaphores. Data moves between devices by JAX's collectives and lax.ppermute only.
A program may use at most 64 MiB of HBM per device.

v0:
```python
import math

import jax
import jax.numpy as jnp
from jax import lax
from jax.sharding import PartitionSpec as P

H = 12
HD = 64


def shifted(block, axis, distance):
    devices = range(lax.axis_size(axis))
    route = [(i - distance, i) for i in devices if i - distance in devices]
    return lax.ppermute(block, axis, route)


def normalize(values):
    values = values.astype(jnp.float32)
    center = jnp.mean(values, axis=-1, keepdims=True)
    spread = jnp.mean((values - center) ** 2, axis=-1, keepdims=True)
    return (values - center) * lax.rsqrt(spread + 1e-05)


def local(slab, tokens, lengths, embed, row_qkv, row_out, col_qkv, col_out):
    slab_rows = slab[0]
    row_lens = lengths[0]
    rows_all = row_lens.shape[0]
    rows_here, length, width = slab_rows.shape
    device_place = lax.axis_index(("depth", "res"))
    my_lens = lax.dynamic_slice_in_dim(row_lens, device_place * rows_here, rows_here)
    positions = jnp.arange(length, dtype=jnp.int32)
    keep_here = positions[None, :] < my_lens[:, None]
    normed = normalize(slab_rows).astype(jnp.bfloat16)
    packed = jnp.dot(
        normed.reshape(-1, width), row_qkv[0], preferred_element_type=jnp.float32
    ).astype(jnp.bfloat16)
    packed = packed.reshape(rows_here, length, 3, H, HD)
    queries = packed[:, :, 0]
    key_rows = packed[:, :, 1]
    key_rows = jnp.where(keep_here[:, :, None, None], key_rows, jnp.zeros_like(key_rows))
    value_rows = packed[:, :, 2]
    partial_logits = jnp.einsum(
        "rihe,rjhe->hij", queries, key_rows, preferred_element_type=jnp.float32
    )
    tied = lax.psum(partial_logits, ("depth", "res")) / math.sqrt(HD * rows_all)
    scores = jnp.where(keep_here[:, None, None, :], tied[None], -1e30)
    weights = jax.nn.softmax(scores, axis=-1).astype(jnp.bfloat16)
    mixed = jnp.einsum(
        "rhij,rjhe->rihe", weights, value_rows, preferred_element_type=jnp.float32
    ).astype(jnp.bfloat16)
    mixed = mixed.reshape(rows_here * length, width)
    after_row = (
        slab_rows.astype(jnp.float32)
        + jnp.dot(mixed, row_out[0], preferred_element_type=jnp.float32).reshape(slab_rows.shape)
    ).astype(jnp.bfloat16)
    normed_col = normalize(after_row).astype(jnp.bfloat16)
    projected = jnp.dot(
        normed_col.reshape(-1, width), col_qkv[0], preferred_element_type=jnp.float32
    ).astype(jnp.bfloat16)
    projected = projected.reshape(rows_here, length, 3 * width)
    regrouped = lax.all_to_all(projected, ("depth", "res"), split_axis=1, concat_axis=0, tiled=True)
    columns = regrouped.shape[1]
    col_parts = regrouped.reshape(rows_all, columns, 3, H, HD)
    col_start = device_place * columns
    residue_here = col_start + jnp.arange(columns, dtype=jnp.int32)
    keep_cols = residue_here[None, :] < row_lens[:, None]
    col_scores = jnp.einsum(
        "rihe,sihe->ihrs",
        col_parts[:, :, 0],
        col_parts[:, :, 1],
        preferred_element_type=jnp.float32,
    ) / math.sqrt(HD)
    col_scores = jnp.where(keep_cols.T[:, None, None, :], col_scores, -1e30)
    col_weights = jax.nn.softmax(col_scores, axis=-1).astype(jnp.bfloat16)
    col_mixed = jnp.einsum(
        "ihrs,sihe->rihe", col_weights, col_parts[:, :, 2], preferred_element_type=jnp.float32
    ).astype(jnp.bfloat16)
    col_mixed = col_mixed.reshape(rows_all, columns, width)
    restored = lax.all_to_all(col_mixed, ("depth", "res"), split_axis=0, concat_axis=1, tiled=True)
    layer_result = after_row.astype(jnp.float32) + jnp.dot(
        restored.reshape(-1, width), col_out[0], preferred_element_type=jnp.float32
    ).reshape(after_row.shape)
    layer_result = layer_result.astype(jnp.bfloat16)
    handed = shifted(layer_result, "section", 1)
    onehot = (
        tokens[:, :, None] == jnp.arange(embed.shape[0], dtype=jnp.int32)[None, None, :]
    ).astype(jnp.bfloat16)
    embedded = jnp.einsum("rlv,vd->rld", onehot, embed, preferred_element_type=jnp.float32).astype(
        jnp.bfloat16
    )
    is_first = lax.axis_index("section") == 0
    return jnp.where(is_first, embedded, handed)[None]


def solution(mesh):
    in_specs = (
        P("section", ("depth", "res"), None, None),
        P(("depth", "res"), None),
        P("section", None),
        P(),
        P("section", None, None),
        P("section", None, None),
        P("section", None, None),
        P("section", None, None),
    )
    out_specs = P("section", ("depth", "res"), None, None)
    return jax.shard_map(local, mesh=mesh, in_specs=in_specs, out_specs=out_specs, check_vma=False)
```

profile of v0, /device:TPU:32, one launch (start us, length us, event | category | flops | bytes accessed | tf_op | source)
XLA Modules:
  0.0 382.5 jit_solution(11806841701829004270)
XLA Ops:
  6.5 0.9 dynamic-slice_bitcast_fusion
  7.5 1.2 convert_reduce_fusion
  8.7 1.2 fusion.23
  9.9 1.2 fusion.25
  11.1 1.9 convolution_convert_fusion.1
  12.9 2.3 copy.40
  15.3 3.9 %reshape.152 = bf16[2,96,3,12,64]{1,0,4,3,2:T(2,128)(2,1)} reshape(bf16[192,2304]{0,1:T(8,128)(2,1)} %copy.40) | data formatting | bytes 1769472 | tf_op jit(solution)/shard_map/reshape | solution.py:38
  19.1 2.6 fusion.43
  21.8 1.3 broadcast_select_fusion
  23.1 1.1 convolution_bitcast_fusion
  24.2 245.4 %all-reduce.2.cloned.1.call-done = f32[12,96,96]{2,1,0:T(8,128)} async-done(((f32[12,96,96]{2,1,0:T(8,128)}), f32[12,96,96]{2,1,0:T(8,128)}) %all-reduce.2.cloned.1.call-update) | async-done | bytes 442384 | tf_op jit(solution)/shard_map/psum | solution.py:46
  269.6 1.1 broadcast_multiply_fusion
  271.5 1.4 fusion.44
  272.9 6.2 %convolution_convert_fusion.3 = bf16[2,12,64,96]{3,2,1,0:T(8,128)(2,1)} fusion(f32[2,12,96]{2,1,0:T(8,128)} %fusion.44, bf16[2,96,1,12,64]{1,0,4,3,2:T(2,128)(2,1)} %get-tuple-element.8, f32[12,96,96]{2,1,0:T(8,128)} %copy-done.3, pred[2,96]{1,0:T(4,128)(4,1)S(1)} %iota_compare_fusion.2), kind=kOutput, calls=%fused_computation.18 | convolution fusion | flops 29567328 | bytes 1041600 | tf_op jit(solution)/shard_map/rhij,rjhe->rihe/dot_general | solution.py:49
  279.2 2.1 fusion.45
  283.1 1.9 copy.45
  285.0 4.9 %all-to-all-start = ((bf16[2,96,2304]{2,0,1:T(2,128)(2,1)}), bf16[2,96,2304]{2,0,1:T(2,128)(2,1)}, u32[]{:S(2)}, u32[]{:S(2)}) async-start(bf16[2,96,2304]{2,0,1:T(2,128)(2,1)} %copy.45), calls=%async_computation | async-start | bytes 1769472 | tf_op jit(solution)/shard_map/all_to_all | solution.py:62
  290.0 23.9 %all-to-all-done = bf16[2,96,2304]{2,0,1:T(2,128)(2,1)} async-done(((bf16[2,96,2304]{2,0,1:T(2,128)(2,1)}), bf16[2,96,2304]{2,0,1:T(2,128)(2,1)}, u32[]{:S(2)}, u32[]{:S(2)}) %all-to-all-start) | async-done | bytes 884768 | tf_op jit(solution)/shard_map/all_to_all | solution.py:62
  313.9 2.4 copy.46
  316.4 3.9 %reshape.155 = bf16[48,4,3,12,64]{4,3,2,1,0:T(8,128)(2,1)} reshape(bf16[24,2,4,2304]{3,2,1,0:T(4,128)(2,1)} %copy.46) | data formatting | bytes 1769472 | tf_op jit(solution)/shard_map/reshape | solution.py:64
  320.3 3.2 fusion.42
  323.5 3.0 fusion.46
  326.5 3.2 fusion.12
  329.7 3.5 fusion.13
  333.2 2.2 copy.57
  335.4 2.5 reshape.161
  337.8 20.1 %all_to_all.30 = bf16[48,4,768]{2,1,0:T(4,128)(2,1)S(1)} all-to-all(bf16[48,4,768]{2,1,0:T(4,128)(2,1)} %reshape.161), channel_id=1, replica_groups=mesh['section'=32,'depth'=2,'res'=12] {'depth','res'}, dimensions={0} | all-to-all | bytes 589824 | tf_op jit(solution)/shard_map/all_to_all | solution.py:80
  358.8 1.7 dot_general.40
  360.5 2.6 fusion.15
  363.2 1.9 collective-permute-start
  365.1 8.5 %collective-permute-done = bf16[2,96,768]{2,1,0:T(8,128)(2,1)} collective-permute-done((bf16[2,96,768]{2,1,0:T(8,128)(2,1)}, bf16[2,96,768]{2,1,0:T(8,128)(2,1)}, u32[]{:S(2)}, u32[]{:S(2)}) %collective-permute-start) | collective-permute-done | bytes 294944 | tf_op jit(solution)/shard_map/ppermute | solution.py:15
  373.6 2.0 fusion.20
  (25 shorter events, 3.6 us)
Async XLA Ops:
  6.5 4.5 %copy-start = (bf16[1,768,2304]{2,1,0:T(8,128)(2,1)S(1)}, bf16[1,768,2304]{2,1,0:T(8,128)(2,1)}, u32[]{:S(2)}) copy-start(bf16[1,768,2304]{2,1,0:T(8,128)(2,1)} %param.12) | copy-start | bytes 10616836
  6.5 263.0 %all-reduce.2.cloned.1.call-start = ((), (), s32[]{:S(2)}) async-start(), calls=%async_computation.2 | async-start | bytes 1179648 | tf_op jit(solution)/shard_map/psum | solution.py:46
  270.7 0.8 copy-start.3
  279.2 3.1 copy-start.2
  281.3 0.8 copy-start.1
  285.0 4.9 %copy-start.5 = (s32[1,48]{1,0:T(1,128)S(1)}, s32[1,48]{1,0:T(1,128)}, u32[]{:S(2)}) copy-start(s32[1,48]{1,0:T(1,128)} %param.10) | copy-start | bytes 580
  285.0 28.9 %all-to-all-start = ((bf16[2,96,2304]{2,0,1:T(2,128)(2,1)}), bf16[2,96,2304]{2,0,1:T(2,128)(2,1)}, u32[]{:S(2)}, u32[]{:S(2)}) async-start(bf16[2,96,2304]{2,0,1:T(2,128)(2,1)} %copy.45), calls=%async_computation | async-start | bytes 1769472 | tf_op jit(solution)/shard_map/all_to_all | solution.py:62
  360.5 13.1 %copy-start.4 = (s32[2,96]{1,0:T(2,128)S(1)}, s32[2,96]{1,0:T(2,128)}, u32[]{:S(2)}) copy-start(s32[2,96]{1,0:T(2,128)} %param.9) | copy-start | bytes 2308
  363.2 10.5 %collective-permute-start = (bf16[2,96,768]{2,1,0:T(8,128)(2,1)}, bf16[2,96,768]{2,1,0:T(8,128)(2,1)}, u32[]{:S(2)}, u32[]{:S(2)}) collective-permute-start(bf16[2,96,768]{2,1,0:T(8,128)(2,1)} %fusion.15), channel_id=1, source_target_pairs={{0,24},{24,48},{48,72},{72,96},{96,120},{120,144},{144,168},{168,1... | collective-permute-start | bytes 884744 | tf_op jit(solution)/shard_map/ppermute | solution.py:15
Sparse Core Ops, SparseCore 0:
  24.3 245.1 all-reduce.1
where the time goes:
time: 383 us; the launch traced here: 382 us
  waiting for transfers between devices  278 us (73%)
  local copies, waits for them, and re-layouts  29.7 us (8%)
  matrix products  26.6 us (7%)
  blocking collectives  20.1 us (5%)
  between operations  13.5 us (4%)
  other arithmetic  7.92 us (2%)
  starting transfers between devices  6.82 us (2%)
    psum x1, waiting for transfers between devices, local(): tied = lax.psum(partial_logits, ('depth', 'res')) / math.sqrt(HD * rows_all)  245 us
    all_to_all x1, waiting for transfers between devices, local(): lax.all_to_all(projected, ('depth', 'res'), split_axis=1, concat_axis=0,...  23.9 us
    all_to_all x1, blocking collectives, local(): lax.all_to_all(col_mixed, ('depth', 'res'), split_axis=0, concat_axis=1,...  20.1 us
    ppermute x1, waiting for transfers between devices, shifted(): return lax.ppermute(block, axis, route)  8.53 us
  transfers between devices with their start and end apart: 3, of which 3 were waited for; matrix products, arithmetic and copies ran while one was open for 0% of the time, Pallas kernels for 0%

commit v1 on v0

v1 whole, which is shorter than its diff:
```python
import functools
import math

import jax
import jax.numpy as jnp
from jax import lax
from jax.experimental import pallas as pl
from jax.experimental.pallas import tpu as pltpu
from jax.sharding import PartitionSpec as P

H = 12
HD = 64
GROUP = ("depth", "res")
SHORTEST = 24
NEG = -1e30
F32 = jnp.float32
BF16 = jnp.bfloat16


def iota(shape, dim):
    return lax.broadcasted_iota(jnp.int32, shape, dim)


def dot(a, b):
    return jnp.dot(a, b, preferred_element_type=F32)


def dot_t(a, b):
    return lax.dot_general(a, b, (((1,), (1,)), ((), ())), preferred_element_type=F32)


def normalize(values):
    values = values.astype(F32)
    center = jnp.mean(values, axis=-1, keepdims=True)
    off = values - center
    spread = jnp.mean(off * off, axis=-1, keepdims=True)
    return (off * lax.rsqrt(spread + 1e-05)).astype(BF16)


def row_length(lens, row):
    return jnp.sum(jnp.where(iota(lens.shape, 1) == row, lens, 0), axis=1, keepdims=True)


def place_of():
    return lax.axis_index(GROUP)


def two_heads(tile):
    first = iota(tile.shape, 1) < HD
    none = jnp.zeros_like(tile)
    return jnp.concatenate([jnp.where(first, tile, none), jnp.where(first, none, tile)], axis=0)


def pick_heads(both):
    n = both.shape[0] // 2
    return jnp.where(iota((n, 2 * HD), 1) < HD, both[:n], both[n:])


def soft(scores):
    top = jnp.max(scores, axis=-1, keepdims=True)
    e = jnp.exp(scores - top)
    return (e * (1.0 / jnp.sum(e, axis=-1, keepdims=True))).astype(BF16)


def row_logits(rows, x_ref, lens_ref, w_ref, part_ref, v_ref):
    n, width = x_ref.shape
    length = n // rows
    packed = dot(normalize(x_ref[...]), w_ref[...]).astype(BF16)
    v_ref[...] = packed[:, 2 * width :]
    place = place_of()
    lens = lens_ref[...]
    keeps = [iota((length, 1), 0) < row_length(lens, place * rows + r) for r in range(rows)]
    for pair in range(H // 2):
        lo = pair * 2 * HD
        q = [packed[r * length : (r + 1) * length, lo : lo + 2 * HD] for r in range(rows)]
        k = [packed[r * length : (r + 1) * length, width + lo : width + lo + 2 * HD] for r in range(rows)]
        k = [jnp.where(keep, part, jnp.zeros_like(part)) for keep, part in zip(keeps, k)]
        wide_q = jnp.concatenate([two_heads(part) for part in q], axis=1)
        wide_k = jnp.concatenate(k, axis=1)
        share = dot_t(wide_q, wide_k)
        part_ref[pair * 2 * length : (pair + 1) * 2 * length, :] = share.astype(part_ref.dtype)


def sum_shares(scale, got_ref, out_ref):
    total = jnp.sum(got_ref[...].astype(F32), axis=0) * scale
    level = jnp.max(total[:, :SHORTEST], axis=1, keepdims=True)
    total = (total - level).astype(out_ref.dtype)
    out_ref[...] = jnp.broadcast_to(total[None], out_ref.shape)


def row_mix(rows, tied_ref, v_ref, x_ref, lens_ref, w_ref, out_ref, mixed_ref):
    n, width = x_ref.shape
    length = n // rows
    place = place_of()
    lens = lens_ref[...]
    for r in range(rows):
        keep = iota((1, length), 1) < row_length(lens, place * rows + r)
        for pair in range(H // 2):
            lo = pair * 2 * HD
            tied = tied_ref[pair * 2 * length : (pair + 1) * 2 * length, :].astype(F32)
            p = soft(jnp.where(keep, tied, NEG))
            both = dot(p, v_ref[r * length : (r + 1) * length, lo : lo + 2 * HD])
            mixed_ref[r * length : (r + 1) * length, lo : lo + 2 * HD] = pick_heads(both).astype(BF16)
    after = (x_ref[...].astype(F32) + dot(mixed_ref[...], w_ref[...])).astype(BF16)
    here, there = iota((n, n), 0), iota((n, n), 1)
    order = (there == (here % rows) * length + here // rows).astype(BF16)
    out_ref[...] = dot(order, after).astype(BF16)


def column_block(rows, x_ref, lens_ref, wqkv_ref, wout_ref, out_ref, mixed_ref):
    n, width = x_ref.shape
    all_rows = lens_ref.shape[1]
    devices = all_rows // rows
    chunk = n // devices
    columns = chunk // rows
    x = x_ref[...]
    packed = dot(normalize(x), wqkv_ref[...]).astype(BF16)
    token = iota((all_rows, n), 1)
    row_of = token // chunk * rows + token % rows
    spread_rows = (row_of == iota((all_rows, n), 0)).astype(BF16)
    lens = jnp.broadcast_to(lens_ref[...].astype(F32), (8, all_rows)).astype(BF16)
    token_lens = dot(lens, spread_rows)[0:1]
    residue_k = iota((n, n), 1) % chunk // rows
    residue_q = iota((n, n), 0) % chunk // rows
    inside = (place_of() * columns + iota((1, n), 1) % chunk // rows).astype(F32) < token_lens
    bias = jnp.where((residue_k == residue_q) & inside, 0.0, NEG)
    bias = jnp.concatenate([bias, bias], axis=0)
    for pair in range(H // 2):
        lo = pair * 2 * HD
        q = two_heads(packed[:, lo : lo + 2 * HD])
        scores = dot_t(q, packed[:, width + lo : width + lo + 2 * HD]) * (1.0 / math.sqrt(HD)) + bias
        both = dot(soft(scores), packed[:, 2 * width + lo : 2 * width + lo + 2 * HD])
        mixed_ref[:, lo : lo + 2 * HD] = pick_heads(both).astype(BF16)
    out_ref[...] = (x.astype(F32) + dot(mixed_ref[...], wout_ref[...])).astype(BF16)


def finish(rows, y_ref, tokens_ref, embed_ref, out_ref):
    n, _ = y_ref.shape
    length = n // rows
    here, there = iota((n, n), 0), iota((n, n), 1)
    order = (there == (here % length) * rows + here // length).astype(BF16)
    handed = dot(order, y_ref[...])
    first = (lax.axis_index("section") == 0).astype(F32)
    table = embed_ref[...]
    for r in range(rows):
        onehot = (iota((table.shape[0], length), 0) == tokens_ref[r : r + 1, :]).astype(F32) * first
        looked = lax.dot_general(
            onehot.astype(BF16), table, (((0,), (0,)), ((), ())), preferred_element_type=F32
        )
        out_ref[r * length : (r + 1) * length, :] = (handed[r * length : (r + 1) * length] + looked).astype(BF16)


def call(body, name, shapes, *operands, scratch=()):
    vmem = pl.BlockSpec(memory_space=pltpu.VMEM)
    return pl.pallas_call(
        body,
        out_shape=shapes,
        in_specs=[vmem] * len(operands),
        out_specs=jax.tree.map(lambda _: vmem, shapes),
        scratch_shapes=list(scratch),
        compiler_params=pltpu.CompilerParams(vmem_limit_bytes=40 * 1024 * 1024),
        name=name,
    )(*operands)


def exchange(blocks):
    return lax.all_to_all(blocks, GROUP, split_axis=0, concat_axis=0, tiled=True)


def local(slab, tokens, lengths, embed, row_qkv, row_out, col_qkv, col_out):
    _, rows, length, width = slab.shape
    all_rows = lengths.shape[1]
    devices = all_rows // rows
    n = rows * length
    piece = H * length // devices
    sds = jax.ShapeDtypeStruct
    x = slab.reshape(n, width)
    shares, values = call(
        functools.partial(row_logits, rows),
        "row_logits",
        (sds((H * length, length), BF16), sds((n, width), BF16)),
        x,
        lengths,
        row_qkv[0],
    )
    got = exchange(shares.reshape(devices, piece, length))
    summed = call(
        functools.partial(sum_shares, 1.0 / math.sqrt(HD * all_rows)),
        "sum_shares",
        sds((devices, piece, length), BF16),
        got,
    )
    tied = exchange(summed).reshape(H * length, length)
    mixed = pltpu.VMEM((n, width), BF16)
    after = call(
        functools.partial(row_mix, rows),
        "row_mix",
        sds((n, width), BF16),
        tied,
        values,
        x,
        lengths,
        row_out[0],
        scratch=[mixed],
    )
    regrouped = exchange(after.reshape(devices, n // devices, width)).reshape(n, width)
    y = call(
        functools.partial(column_block, rows),
        "column_block",
        sds((n, width), BF16),
        regrouped,
        lengths,
        col_qkv[0],
        col_out[0],
        scratch=[mixed],
    )
    sections = lax.axis_size("section")
    handed = lax.ppermute(y, "section", [(s, s + 1) for s in range(sections - 1)])
    restored = exchange(handed.reshape(devices, n // devices, width)).reshape(n, width)
    out = call(
        functools.partial(finish, rows),
        "finish",
        sds((n, width), BF16),
        restored,
        tokens,
        embed,
    )
    return out.reshape(slab.shape)


def solution(mesh):
    in_specs = (
        P("section", ("depth", "res"), None, None),
        P(("depth", "res"), None),
        P("section", None),
        P(),
        P("section", None, None),
        P("section", None, None),
        P("section", None, None),
        P("section", None, None),
    )
    out_specs = P("section", ("depth", "res"), None, None)
    return jax.shard_map(local, mesh=mesh, in_specs=in_specs, out_specs=out_specs, check_vma=False)
```

time: 383 us -> 123 us (0.32)
  the two profiles are of different devices: /device:TPU:32 before, /device:TPU:27 now
where the time goes in v1:
time: 123 us; the launch traced here: 122 us
  blocking collectives  98.9 us (80%)
  starting transfers between devices  9.52 us (8%)
  Pallas kernels  6.57 us (5%)
  local copies, waits for them, and re-layouts  3.65 us (3%)
  waiting for transfers between devices  3.65 us (3%)
    all_to_all x4, blocking collectives, exchange(): lax.all_to_all(blocks, GROUP, split_axis=0, concat_axis=0, tiled=True)  98.9 us
    ppermute x1, starting transfers between devices, local(): lax.ppermute(y, 'section', [(s, s + 1) for s in range(sections - 1)])  9.52 us
    pallas_call x5, Pallas kernels, call(): pl.pallas_call(body, out_shape=shapes, in_specs=[vmem] * len(operands), o...  6.57 us
    unnamed x20, local copies, waits for them, and re-layouts  3.65 us
    ppermute x1, waiting for transfers between devices, local(): lax.ppermute(y, 'section', [(s, s + 1) for s in range(sections - 1)])  3.65 us
  transfers between devices with their start and end apart: 1, of which 1 were waited for; matrix products, arithmetic and copies ran while one was open for 0% of the time, Pallas kernels for 0%

profile of v1, /device:TPU:27, one launch (start us, length us, event | category | flops | bytes accessed | tf_op | source)
XLA Modules:
  0.0 122.4 jit_solution(17994034888302277066)
XLA Ops:
  0.0 0.0 copy-start
  0.0 2.0 %copy-done = bf16[1,768,2304]{2,1,0:T(8,128)(2,1)S(1)} copy-done((bf16[1,768,2304]{2,1,0:T(8,128)(2,1)S(1)}, bf16[1,768,2304]{2,1,0:T(8,128)(2,1)}, u32[]{:S(2)}) %copy-start) | copy-done | bytes 3538968
  2.0 0.0 copy-start.2
  2.0 1.0 copy-done.2
  3.0 0.0 copy-start.7
  3.0 0.7 copy-done.7
  3.6 0.0 copy-start.3
  3.6 0.0 copy-start.4
  3.6 0.0 copy-start.1
  3.6 0.0 copy-start.5
  3.6 0.0 copy-start.8
  3.6 1.2 row_logits.1
  4.8 32.9 %all_to_all.20.got_ref = bf16[24,48,96]{2,1,0:T(8,128)(2,1)S(1)} all-to-all(bf16[24,48,96]{2,1,0:T(8,128)(2,1)S(1)} %bitcast.22), channel_id=1, replica_groups=mesh['section'=32,'depth'=2,'res'=12] {'depth','res'}, dimensions={0} | all-to-all | bytes 442368 | tf_op jit(solution)/shard_map/all_to_all | solution.py:167
  37.8 0.2 sum_shares.1
  37.9 20.8 %all_to_all.21 = bf16[24,48,96]{2,1,0:T(8,128)(2,1)S(1)} all-to-all(bf16[24,48,96]{2,1,0:T(8,128)(2,1)S(1)} %sum_shares.1), channel_id=1, replica_groups=mesh['section'=32,'depth'=2,'res'=12] {'depth','res'}, dimensions={0} | all-to-all | bytes 442368 | tf_op jit(solution)/shard_map/all_to_all | solution.py:167
  58.7 0.0 copy-done.3
  58.8 0.0 copy-done.4
  58.8 1.4 %row_mix.1 = bf16[192,768]{1,0:T(8,128)(2,1)S(1)} custom-call(bf16[1152,96]{1,0:T(8,128)(2,1)S(1)} %bitcast.16, bf16[192,768]{1,0:T(8,128)(2,1)S(1)} %get-tuple-element.8.v_ref, bf16[192,768]{1,0:T(8,128)(2,1)S(1)} %bitcast.15, s32[1,48]{1,0:T(1,128)S(1)} %copy-done.7, bf16[768,768]{1,0:T(8,128)(2,1)S(1)} %bitcast.19), custom_call_target="tpu_custom_call" | custom-call | tf_op jit(solution)/shard_map/row_mix/pallas_call | solution.py:155
  60.2 0.0 copy-start.6
  60.2 0.0 copy-start.9
  60.2 22.5 %all_to_all.22 = bf16[24,8,768]{2,1,0:T(8,128)(2,1)S(1)} all-to-all(bf16[24,8,768]{2,1,0:T(8,128)(2,1)S(1)} %bitcast.17), channel_id=1, replica_groups=mesh['section'=32,'depth'=2,'res'=12] {'depth','res'}, dimensions={0} | all-to-all | bytes 589824 | tf_op jit(solution)/shard_map/all_to_all | solution.py:167
  82.7 0.0 copy-done.1
  82.7 0.0 copy-done.5
  82.7 0.0 copy-done.8
  82.7 2.8 %column_block.1 = bf16[192,768]{1,0:T(8,128)(2,1)S(1)} custom-call(bf16[192,768]{1,0:T(8,128)(2,1)S(1)} %bitcast.18, s32[1,48]{1,0:T(1,128)S(1)} %copy-done.8, bf16[768,2304]{1,0:T(8,128)(2,1)S(1)} %bitcast.13, bf16[768,768]{1,0:T(8,128)(2,1)S(1)} %bitcast.21), custom_call_target="tpu_custom_call" | custom-call | tf_op jit(solution)/shard_map/column_block/pallas_call | solution.py:155
  85.5 9.5 %collective-permute-start = (bf16[192,768]{1,0:T(8,128)(2,1)S(1)}, bf16[192,768]{1,0:T(8,128)(2,1)S(1)}, u32[]{:S(2)}, u32[]{:S(2)}) collective-permute-start(bf16[192,768]{1,0:T(8,128)(2,1)S(1)} %column_block.1), channel_id=1, source_target_pairs={{0,24},{24,48},{48,72},{72,96},{96,120},{120,144},{144,168},{168,1... | collective-permute-start | bytes 884744 | tf_op jit(solution)/shard_map/ppermute | solution.py:218
  95.0 3.6 %collective-permute-done = bf16[192,768]{1,0:T(8,128)(2,1)S(1)} collective-permute-done((bf16[192,768]{1,0:T(8,128)(2,1)S(1)}, bf16[192,768]{1,0:T(8,128)(2,1)S(1)}, u32[]{:S(2)}, u32[]{:S(2)}) %collective-permute-start) | collective-permute-done | bytes 294944 | tf_op jit(solution)/shard_map/ppermute | solution.py:218
  98.7 22.7 %all_to_all.23 = bf16[24,8,768]{2,1,0:T(8,128)(2,1)S(1)} all-to-all(bf16[24,8,768]{2,1,0:T(8,128)(2,1)S(1)} %bitcast.23), channel_id=1, replica_groups=mesh['section'=32,'depth'=2,'res'=12] {'depth','res'}, dimensions={0} | all-to-all | bytes 589824 | tf_op jit(solution)/shard_map/all_to_all | solution.py:167
  121.3 0.0 copy-done.6
  121.3 0.0 copy-done.9
  121.3 1.0 finish.1
Async XLA Ops:
  0.0 2.0 %copy-start = (bf16[1,768,2304]{2,1,0:T(8,128)(2,1)S(1)}, bf16[1,768,2304]{2,1,0:T(8,128)(2,1)}, u32[]{:S(2)}) copy-start(bf16[1,768,2304]{2,1,0:T(8,128)(2,1)} %param.12) | copy-start | bytes 10616836
  2.0 1.0 copy-start.2
  3.0 0.7 copy-start.7
  3.6 55.1 %copy-start.3 = (bf16[1,2,96,768]{3,2,1,0:T(8,128)(2,1)S(1)}, bf16[1,2,96,768]{3,2,1,0:T(8,128)(2,1)}, u32[]{:S(2)}) copy-start(bf16[1,2,96,768]{3,2,1,0:T(8,128)(2,1)} %param.8) | copy-start | bytes 884740
  3.6 55.1 %copy-start.4 = (bf16[1,768,768]{2,1,0:T(8,128)(2,1)S(1)}, bf16[1,768,768]{2,1,0:T(8,128)(2,1)}, u32[]{:S(2)}) copy-start(bf16[1,768,768]{2,1,0:T(8,128)(2,1)} %param.13) | copy-start | bytes 3538948
  3.6 79.1 %copy-start.1 = (bf16[1,768,2304]{2,1,0:T(8,128)(2,1)S(1)}, bf16[1,768,2304]{2,1,0:T(8,128)(2,1)}, u32[]{:S(2)}) copy-start(bf16[1,768,2304]{2,1,0:T(8,128)(2,1)} %param.14) | copy-start | bytes 10616836
  3.6 79.1 %copy-start.5 = (bf16[1,768,768]{2,1,0:T(8,128)(2,1)S(1)}, bf16[1,768,768]{2,1,0:T(8,128)(2,1)}, u32[]{:S(2)}) copy-start(bf16[1,768,768]{2,1,0:T(8,128)(2,1)} %param.15) | copy-start | bytes 3538948
  3.6 79.1 %copy-start.8 = (s32[1,48]{1,0:T(1,128)S(1)}, s32[1,48]{1,0:T(1,128)}, u32[]{:S(2)}) copy-start(s32[1,48]{1,0:T(1,128)} %lens_ref.5) | copy-start | bytes 580
  60.2 61.2 %copy-start.6 = (bf16[33,768]{1,0:T(8,128)(2,1)S(1)}, bf16[33,768]{1,0:T(8,128)(2,1)}, u32[]{:S(2)}) copy-start(bf16[33,768]{1,0:T(8,128)(2,1)} %embed_ref.1) | copy-start | bytes 152068
  60.2 61.2 %copy-start.9 = (s32[2,96]{1,0:T(2,128)S(1)}, s32[2,96]{1,0:T(2,128)}, u32[]{:S(2)}) copy-start(s32[2,96]{1,0:T(2,128)} %tokens_ref.1) | copy-start | bytes 2308
  85.5 13.2 %collective-permute-start = (bf16[192,768]{1,0:T(8,128)(2,1)S(1)}, bf16[192,768]{1,0:T(8,128)(2,1)S(1)}, u32[]{:S(2)}, u32[]{:S(2)}) collective-permute-start(bf16[192,768]{1,0:T(8,128)(2,1)S(1)} %column_block.1), channel_id=1, source_target_pairs={{0,24},{24,48},{48,72},{72,96},{96,120},{120,144},{144,168},{168,1... | collective-permute-start | bytes 884744 | tf_op jit(solution)/shard_map/ppermute | solution.py:218

commit v2 on v1

--- a/solution.py
+++ b/solution.py
@@ -12,6 +12,11 @@
 HD = 64
 GROUP = ("depth", "res")
 SHORTEST = 24
+DELAY = 3000
+ALL_VMEM = 67_043_328
+ROOM = 20_000_000
+ROOM_LOGITS = 3_000_000
+COVER = 4_000_000_000
 NEG = -1e30
 F32 = jnp.float32
 BF16 = jnp.bfloat16
@@ -37,10 +42,6 @@
     return (off * lax.rsqrt(spread + 1e-05)).astype(BF16)
 
 
-def row_length(lens, row):
-    return jnp.sum(jnp.where(iota(lens.shape, 1) == row, lens, 0), axis=1, keepdims=True)
-
-
 def place_of():
     return lax.axis_index(GROUP)
 
@@ -62,14 +63,56 @@
     return (e * (1.0 / jnp.sum(e, axis=-1, keepdims=True))).astype(BF16)
 
 
-def row_logits(rows, x_ref, lens_ref, w_ref, part_ref, v_ref):
-    n, width = x_ref.shape
+def pack(block):
+    m = block.shape[0] // 2
+    third = block.shape[0] // 3
+    left, right = block[:, :HD], block[:, HD:]
+    wide = jnp.concatenate([left[:m], left[m:]], axis=1)
+    rest = [right[i * third : (i + 1) * third] for i in range(3)]
+    rest = jnp.concatenate(rest + [jnp.zeros_like(rest[0])], axis=1)
+    return jnp.concatenate([wide, rest], axis=0)
+
+
+def unpack(block):
+    m = block.shape[0] * 3 // 5
+    wide, rest = block[:m], block[m:]
+    left = jnp.concatenate([wide[:, :HD], wide[:, HD:]], axis=0)
+    right = jnp.concatenate([rest[:, :32], rest[:, 32:64], rest[:, 64:96]], axis=0)
+    return jnp.concatenate([left, right], axis=1)
+
+
+def own_lengths(lens, rows):
+    row = lax.axis_index(GROUP) * rows + iota((rows, lens.shape[1]), 0)
+    return jnp.sum(jnp.where(iota(row.shape, 1) == row, lens, 0), axis=1, keepdims=True)
+
+
+def row_logits(rows, x_hbm, lens_hbm, w_hbm, part_ref, v_ref, x_ref, lens_ref, w_ref, sems):
+    n, width = x_hbm.shape
     length = n // rows
-    packed = dot(normalize(x_ref[...]), w_ref[...]).astype(BF16)
-    v_ref[...] = packed[:, 2 * width :]
-    place = place_of()
-    lens = lens_ref[...]
-    keeps = [iota((length, 1), 0) < row_length(lens, place * rows + r) for r in range(rows)]
+    parts = w_ref.shape[0]
+    copies = [
+        pltpu.make_async_copy(w_hbm.at[:, pl.ds(i * width, width)], w_ref.at[i], sems.at[i])
+        for i in range(parts)
+    ]
+    copy_x = pltpu.make_async_copy(x_hbm, x_ref, sems.at[parts])
+    copy_lens = pltpu.make_async_copy(lens_hbm, lens_ref, sems.at[parts + 1])
+    for copy in [copy_x, copy_lens] + copies:
+        copy.start()
+
+    @pl.when(lax.axis_index("section") % 2 == 0)
+    def _():
+        pl.delay(DELAY)
+
+    copy_lens.wait()
+    mine = own_lengths(lens_ref[...], rows)
+    copy_x.wait()
+    normed = normalize(x_ref[...])
+    packed = []
+    for i, copy in enumerate(copies[:2]):
+        copy.wait()
+        packed.append(dot(normed, w_ref[i]).astype(BF16))
+    packed = jnp.concatenate(packed, axis=1)
+    keeps = [iota((length, 1), 0) < mine[r : r + 1] for r in range(rows)]
     for pair in range(H // 2):
         lo = pair * 2 * HD
         q = [packed[r * length : (r + 1) * length, lo : lo + 2 * HD] for r in range(rows)]
@@ -78,30 +121,36 @@
         wide_q = jnp.concatenate([two_heads(part) for part in q], axis=1)
         wide_k = jnp.concatenate(k, axis=1)
         share = dot_t(wide_q, wide_k)
-        part_ref[pair * 2 * length : (pair + 1) * 2 * length, :] = share.astype(part_ref.dtype)
+        half = length // 2
+        for i in range(4):
+            part_ref[pair * 4 + i] = pack(share[i * half : (i + 1) * half]).astype(part_ref.dtype)
+    copies[2].wait()
+    v_ref[...] = dot(normed, w_ref[2]).astype(BF16)
 
 
 def sum_shares(scale, got_ref, out_ref):
-    total = jnp.sum(got_ref[...].astype(F32), axis=0) * scale
+    total = unpack(jnp.sum(got_ref[...].astype(F32), axis=0) * scale)
     level = jnp.max(total[:, :SHORTEST], axis=1, keepdims=True)
-    total = (total - level).astype(out_ref.dtype)
+    total = pack(total - level).astype(out_ref.dtype)
     out_ref[...] = jnp.broadcast_to(total[None], out_ref.shape)
 
 
-def row_mix(rows, tied_ref, v_ref, x_ref, lens_ref, w_ref, out_ref, mixed_ref):
+def row_mix(rows, tied_ref, v_ref, x_ref, lens_ref, wout_ref, out_ref, mixed_ref):
     n, width = x_ref.shape
     length = n // rows
-    place = place_of()
-    lens = lens_ref[...]
+    mine = own_lengths(lens_ref[...], rows)
+    tied = [
+        jnp.concatenate([unpack(tied_ref[pair * 4 + i].astype(F32)) for i in range(4)], axis=0)
+        for pair in range(H // 2)
+    ]
     for r in range(rows):
-        keep = iota((1, length), 1) < row_length(lens, place * rows + r)
+        keep = iota((1, length), 1) < mine[r : r + 1]
         for pair in range(H // 2):
             lo = pair * 2 * HD
-            tied = tied_ref[pair * 2 * length : (pair + 1) * 2 * length, :].astype(F32)
-            p = soft(jnp.where(keep, tied, NEG))
+            p = soft(jnp.where(keep, tied[pair], NEG))
             both = dot(p, v_ref[r * length : (r + 1) * length, lo : lo + 2 * HD])
             mixed_ref[r * length : (r + 1) * length, lo : lo + 2 * HD] = pick_heads(both).astype(BF16)
-    after = (x_ref[...].astype(F32) + dot(mixed_ref[...], w_ref[...])).astype(BF16)
+    after = (x_ref[...].astype(F32) + dot(mixed_ref[...], wout_ref[...])).astype(BF16)
     here, there = iota((n, n), 0), iota((n, n), 1)
     order = (there == (here % rows) * length + here // rows).astype(BF16)
     out_ref[...] = dot(order, after).astype(BF16)
@@ -137,28 +186,36 @@
 def finish(rows, y_ref, tokens_ref, embed_ref, out_ref):
     n, _ = y_ref.shape
     length = n // rows
-    here, there = iota((n, n), 0), iota((n, n), 1)
-    order = (there == (here % length) * rows + here // length).astype(BF16)
-    handed = dot(order, y_ref[...])
-    first = (lax.axis_index("section") == 0).astype(F32)
-    table = embed_ref[...]
-    for r in range(rows):
-        onehot = (iota((table.shape[0], length), 0) == tokens_ref[r : r + 1, :]).astype(F32) * first
-        looked = lax.dot_general(
-            onehot.astype(BF16), table, (((0,), (0,)), ((), ())), preferred_element_type=F32
-        )
-        out_ref[r * length : (r + 1) * length, :] = (handed[r * length : (r + 1) * length] + looked).astype(BF16)
-
-
-def call(body, name, shapes, *operands, scratch=()):
+    last = lax.axis_index("section") == lax.axis_size("section") - 1
+
+    @pl.when(jnp.logical_not(last))
+    def _():
+        here, there = iota((n, n), 0), iota((n, n), 1)
+        order = (there == (here % length) * rows + here // length).astype(BF16)
+        out_ref[...] = dot(order, y_ref[...]).astype(BF16)
+
+    @pl.when(last)
+    def _():
+        table = embed_ref[...]
+        for r in range(rows):
+            onehot = (iota((table.shape[0], length), 0) == tokens_ref[r : r + 1, :]).astype(BF16)
+            looked = lax.dot_general(
+                onehot, table, (((0,), (0,)), ((), ())), preferred_element_type=F32
+            )
+            out_ref[r * length : (r + 1) * length, :] = looked.astype(BF16)
+
+
+def call(body, name, shapes, *operands, scratch=(), far=(), room=ROOM, cost=None):
     vmem = pl.BlockSpec(memory_space=pltpu.VMEM)
+    hbm = pl.BlockSpec(memory_space=pltpu.HBM)
     return pl.pallas_call(
         body,
         out_shape=shapes,
-        in_specs=[vmem] * len(operands),
+        in_specs=[hbm if i in far else vmem for i in range(len(operands))],
         out_specs=jax.tree.map(lambda _: vmem, shapes),
         scratch_shapes=list(scratch),
-        compiler_params=pltpu.CompilerParams(vmem_limit_bytes=40 * 1024 * 1024),
+        compiler_params=pltpu.CompilerParams(vmem_limit_bytes=ALL_VMEM - room),
+        cost_estimate=cost,
         name=name,
     )(*operands)
 
@@ -172,25 +229,34 @@
     all_rows = lengths.shape[1]
     devices = all_rows // rows
     n = rows * length
-    piece = H * length // devices
+    piece = length // 4 + 16
     sds = jax.ShapeDtypeStruct
     x = slab.reshape(n, width)
     shares, values = call(
         functools.partial(row_logits, rows),
         "row_logits",
-        (sds((H * length, length), BF16), sds((n, width), BF16)),
+        (sds((devices, piece, 2 * HD), BF16), sds((n, width), BF16)),
         x,
         lengths,
         row_qkv[0],
-    )
-    got = exchange(shares.reshape(devices, piece, length))
+        far=(0, 1, 2),
+        room=ROOM_LOGITS,
+        scratch=[
+            pltpu.VMEM((n, width), BF16),
+            pltpu.VMEM(lengths.shape, jnp.int32),
+            pltpu.VMEM((3, width, width), BF16),
+            pltpu.SemaphoreType.DMA((5,)),
+        ],
+    )
+    got = exchange(shares)
     summed = call(
         functools.partial(sum_shares, 1.0 / math.sqrt(HD * all_rows)),
         "sum_shares",
-        sds((devices, piece, length), BF16),
+        sds((devices, piece, 2 * HD), BF16),
         got,
-    )
-    tied = exchange(summed).reshape(H * length, length)
+        cost=pl.CostEstimate(flops=COVER, bytes_accessed=0, transcendentals=0),
+    )
+    tied = exchange(summed)
     mixed = pltpu.VMEM((n, width), BF16)
     after = call(
         functools.partial(row_mix, rows),
@@ -214,9 +280,7 @@
         col_out[0],
         scratch=[mixed],
     )
-    sections = lax.axis_size("section")
-    handed = lax.ppermute(y, "section", [(s, s + 1) for s in range(sections - 1)])
-    restored = exchange(handed.reshape(devices, n // devices, width)).reshape(n, width)
+    restored = exchange(y.reshape(devices, n // devices, width)).reshape(n, width)
     out = call(
         functools.partial(finish, rows),
         "finish",
@@ -225,6 +289,8 @@
         tokens,
         embed,
     )
+    sections = lax.axis_size("section")
+    out = lax.ppermute(out, "section", [(s, (s + 1) % sections) for s in range(sections)])
     return out.reshape(slab.shape)
 
 

time: 123 us -> 113 us (0.919)
  the two profiles are of different devices: /device:TPU:27 before, /device:TPU:32 now
where the time goes in v2:
time: 113 us
  blocking collectives  90.8 us (80%)
  Pallas kernels  10.8 us (10%)
  waiting for transfers between devices  8.22 us (7%)
  starting transfers between devices  1.92 us (2%)
    all_to_all x4, blocking collectives, exchange(): lax.all_to_all(blocks, GROUP, split_axis=0, concat_axis=0, tiled=True)  90.8 us
    pallas_call x5, Pallas kernels, call(): pl.pallas_call(body, out_shape=shapes, in_specs=[hbm if i in far else vme...  10.8 us
    ppermute x1, waiting for transfers between devices, local(): lax.ppermute(out, 'section', [(s, (s + 1) % sections) for s in range(sect...  8.22 us
  transfers between devices with their start and end apart: 1, of which 1 were waited for; matrix products, arithmetic and copies ran while one was open for 0% of the time, Pallas kernels for 0%

profile of v2, /device:TPU:32, one launch (start us, length us, event | category | flops | bytes accessed | tf_op | source)
XLA Modules:
  0.0 112.6 jit_solution(16930877426349539181)
XLA Ops:
  0.0 5.7 %row_logits.1 = (bf16[24,40,128]{2,1,0:T(8,128)(2,1)}, bf16[192,768]{1,0:T(8,128)(2,1)}) custom-call(bf16[192,768]{1,0:T(8,128)(2,1)} %bitcast.11, s32[1,48]{1,0:T(1,128)} %lens_ref.3, bf16[768,2304]{1,0:T(8,128)(2,1)} %bitcast.19), custom_call_target="tpu_custom_call" | custom-call | tf_op jit(solution)/shard_map/row_logits/pallas_call | solution.py:211
  5.7 33.4 %all_to_all.20.got_ref = bf16[24,40,128]{2,1,0:T(8,128)(2,1)S(1)} all-to-all(bf16[24,40,128]{2,1,0:T(8,128)(2,1)} %get-tuple-element.7), channel_id=1, replica_groups=mesh['section'=32,'depth'=2,'res'=12] {'depth','res'}, dimensions={0} | all-to-all | bytes 491520 | tf_op jit(solution)/shard_map/all_to_all | solution.py:224
  39.2 0.0 copy-start.1
  39.2 0.0 copy-start.2
  39.2 0.0 copy-start.4
  39.2 0.0 copy-start.6
  39.2 0.0 copy-start
  39.2 0.3 sum_shares.1
  39.5 0.0 copy-start.3
  39.5 19.0 %all_to_all.21.tied_ref = bf16[24,40,128]{2,1,0:T(8,128)(2,1)S(1)} all-to-all(bf16[24,40,128]{2,1,0:T(8,128)(2,1)S(1)} %sum_shares.1), channel_id=1, replica_groups=mesh['section'=32,'depth'=2,'res'=12] {'depth','res'}, dimensions={0} | all-to-all | bytes 491520 | tf_op jit(solution)/shard_map/all_to_all | solution.py:224
  58.5 0.0 copy-done.1
  58.5 0.0 copy-done.2
  58.5 0.0 copy-done.4
  58.5 0.0 copy-done.6
  58.5 1.7 %row_mix.1 = bf16[192,768]{1,0:T(8,128)(2,1)S(1)} custom-call(bf16[24,40,128]{2,1,0:T(8,128)(2,1)S(1)} %all_to_all.21.tied_ref, bf16[192,768]{1,0:T(8,128)(2,1)S(1)} %copy-done.4, bf16[192,768]{1,0:T(8,128)(2,1)S(1)} %bitcast.12, s32[1,48]{1,0:T(1,128)S(1)} %copy-done.6, bf16[768,768]{1,0:T(8,128)(2,1)S(1)} %bitcast.16), custom_call_target="tpu_custom_call" | custom-call | tf_op jit(solution)/shard_map/row_mix/pallas_call | solution.py:211
  60.3 0.0 copy-start.5
  60.3 0.0 copy-start.7
  60.3 20.1 %all_to_all.22 = bf16[24,8,768]{2,1,0:T(8,128)(2,1)S(1)} all-to-all(bf16[24,8,768]{2,1,0:T(8,128)(2,1)S(1)} %bitcast.13), channel_id=1, replica_groups=mesh['section'=32,'depth'=2,'res'=12] {'depth','res'}, dimensions={0} | all-to-all | bytes 589824 | tf_op jit(solution)/shard_map/all_to_all | solution.py:224
  80.4 0.0 copy-done
  80.4 0.0 copy-done.3
  80.4 2.8 %column_block.1 = bf16[192,768]{1,0:T(8,128)(2,1)S(1)} custom-call(bf16[192,768]{1,0:T(8,128)(2,1)S(1)} %bitcast.14, s32[1,48]{1,0:T(1,128)S(1)} %copy-done.6, bf16[768,2304]{1,0:T(8,128)(2,1)S(1)} %bitcast.10, bf16[768,768]{1,0:T(8,128)(2,1)S(1)} %bitcast.18), custom_call_target="tpu_custom_call" | custom-call | tf_op jit(solution)/shard_map/column_block/pallas_call | solution.py:211
  83.2 18.3 %all_to_all.23 = bf16[24,8,768]{2,1,0:T(8,128)(2,1)S(1)} all-to-all(bf16[24,8,768]{2,1,0:T(8,128)(2,1)S(1)} %bitcast.15), channel_id=1, replica_groups=mesh['section'=32,'depth'=2,'res'=12] {'depth','res'}, dimensions={0} | all-to-all | bytes 589824 | tf_op jit(solution)/shard_map/all_to_all | solution.py:224
  101.5 0.0 copy-done.5
  101.5 0.0 copy-done.7
  101.5 0.2 finish.1
  101.7 1.9 %collective-permute-start = (bf16[192,768]{1,0:T(8,128)(2,1)S(1)}, bf16[192,768]{1,0:T(8,128)(2,1)S(1)}, u32[]{:S(2)}, u32[]{:S(2)}) collective-permute-start(bf16[192,768]{1,0:T(8,128)(2,1)S(1)} %finish.1), channel_id=1, source_target_pairs={{0,24},{24,48},{48,72},{72,96},{96,120},{120,144},{144,168},{168,1... | collective-permute-start | bytes 884744 | tf_op jit(solution)/shard_map/ppermute | solution.py:293
  103.7 8.2 %collective-permute-done = bf16[192,768]{1,0:T(8,128)(2,1)S(1)} collective-permute-done((bf16[192,768]{1,0:T(8,128)(2,1)S(1)}, bf16[192,768]{1,0:T(8,128)(2,1)S(1)}, u32[]{:S(2)}, u32[]{:S(2)}) %collective-permute-start) | collective-permute-done | bytes 294944 | tf_op jit(solution)/shard_map/ppermute | solution.py:293
  111.9 0.7 copy.10
Async XLA Ops:
  39.2 19.3 %copy-start.1 = (bf16[1,2,96,768]{3,2,1,0:T(8,128)(2,1)S(1)}, bf16[1,2,96,768]{3,2,1,0:T(8,128)(2,1)}, u32[]{:S(2)}) copy-start(bf16[1,2,96,768]{3,2,1,0:T(8,128)(2,1)} %param.8) | copy-start | bytes 884740
  39.2 19.4 %copy-start.2 = (bf16[1,768,768]{2,1,0:T(8,128)(2,1)S(1)}, bf16[1,768,768]{2,1,0:T(8,128)(2,1)}, u32[]{:S(2)}) copy-start(bf16[1,768,768]{2,1,0:T(8,128)(2,1)} %param.13) | copy-start | bytes 3538948
  39.2 19.4 %copy-start.4 = (bf16[192,768]{1,0:T(8,128)(2,1)S(1)}, bf16[192,768]{1,0:T(8,128)(2,1)}, u32[]{:S(2)}) copy-start(bf16[192,768]{1,0:T(8,128)(2,1)} %get-tuple-element.8.v_ref) | copy-start | bytes 884740
  39.2 19.4 %copy-start.6 = (s32[1,48]{1,0:T(1,128)S(1)}, s32[1,48]{1,0:T(1,128)}, u32[]{:S(2)}) copy-start(s32[1,48]{1,0:T(1,128)} %lens_ref.3) | copy-start | bytes 580
  39.2 41.2 %copy-start = (bf16[1,768,2304]{2,1,0:T(8,128)(2,1)S(1)}, bf16[1,768,2304]{2,1,0:T(8,128)(2,1)}, u32[]{:S(2)}) copy-start(bf16[1,768,2304]{2,1,0:T(8,128)(2,1)} %param.14) | copy-start | bytes 10616836
  39.5 40.9 %copy-start.3 = (bf16[1,768,768]{2,1,0:T(8,128)(2,1)S(1)}, bf16[1,768,768]{2,1,0:T(8,128)(2,1)}, u32[]{:S(2)}) copy-start(bf16[1,768,768]{2,1,0:T(8,128)(2,1)} %param.15) | copy-start | bytes 3538948
  60.3 41.2 %copy-start.5 = (bf16[33,768]{1,0:T(8,128)(2,1)S(1)}, bf16[33,768]{1,0:T(8,128)(2,1)}, u32[]{:S(2)}) copy-start(bf16[33,768]{1,0:T(8,128)(2,1)} %embed_ref.1) | copy-start | bytes 152068
  60.3 41.2 %copy-start.7 = (s32[2,96]{1,0:T(2,128)S(1)}, s32[2,96]{1,0:T(2,128)}, u32[]{:S(2)}) copy-start(s32[2,96]{1,0:T(2,128)} %tokens_ref.1) | copy-start | bytes 2308
  101.7 10.2 %collective-permute-start = (bf16[192,768]{1,0:T(8,128)(2,1)S(1)}, bf16[192,768]{1,0:T(8,128)(2,1)S(1)}, u32[]{:S(2)}, u32[]{:S(2)}) collective-permute-start(bf16[192,768]{1,0:T(8,128)(2,1)S(1)} %finish.1), channel_id=1, source_target_pairs={{0,24},{24,48},{48,72},{72,96},{96,120},{120,144},{144,168},{168,1... | collective-permute-start | bytes 884744 | tf_op jit(solution)/shard_map/ppermute | solution.py:293

commit v3 on v2

--- a/solution.py
+++ b/solution.py
@@ -61,6 +61,13 @@
     top = jnp.max(scores, axis=-1, keepdims=True)
     e = jnp.exp(scores - top)
     return (e * (1.0 / jnp.sum(e, axis=-1, keepdims=True))).astype(BF16)
+
+
+def attend(scores, values):
+    weights = jnp.exp(scores - jnp.max(scores, axis=-1, keepdims=True)).astype(BF16)
+    width = values.shape[1]
+    both = dot(weights, jnp.concatenate([values, jnp.ones_like(values)], axis=1))
+    return both[:, :width] * (1.0 / both[:, width:])
 
 
 def pack(block):
@@ -176,9 +183,9 @@
     bias = jnp.concatenate([bias, bias], axis=0)
     for pair in range(H // 2):
         lo = pair * 2 * HD
-        q = two_heads(packed[:, lo : lo + 2 * HD])
-        scores = dot_t(q, packed[:, width + lo : width + lo + 2 * HD]) * (1.0 / math.sqrt(HD)) + bias
-        both = dot(soft(scores), packed[:, 2 * width + lo : 2 * width + lo + 2 * HD])
+        q = two_heads(packed[:, lo : lo + 2 * HD] * jnp.asarray(1.0 / math.sqrt(HD), BF16))
+        scores = dot_t(q, packed[:, width + lo : width + lo + 2 * HD]) + bias
+        both = attend(scores, packed[:, 2 * width + lo : 2 * width + lo + 2 * HD])
         mixed_ref[:, lo : lo + 2 * HD] = pick_heads(both).astype(BF16)
     out_ref[...] = (x.astype(F32) + dot(mixed_ref[...], wout_ref[...])).astype(BF16)
 

time: 113 us -> 113 us (level)
  no operation moved by 1% of the time
where the time goes in v3:
time: 113 us; the launch traced here: 112 us
  blocking collectives  90.8 us (80%)
  Pallas kernels  10.4 us (9%)
  waiting for transfers between devices  8.22 us (7%)
  starting transfers between devices  1.92 us (2%)
    all_to_all x4, blocking collectives, exchange(): lax.all_to_all(blocks, GROUP, split_axis=0, concat_axis=0, tiled=True)  90.8 us
    pallas_call x5, Pallas kernels, call(): pl.pallas_call(body, out_shape=shapes, in_specs=[hbm if i in far else vme...  10.4 us
    ppermute x1, waiting for transfers between devices, local(): lax.ppermute(out, 'section', [(s, (s + 1) % sections) for s in range(sect...  8.22 us
  transfers between devices with their start and end apart: 1, of which 1 were waited for; matrix products, arithmetic and copies ran while one was open for 0% of the time, Pallas kernels for 0%

profile of v3, /device:TPU:32, one launch (start us, length us, event | category | flops | bytes accessed | tf_op | source)
XLA Modules:
  0.0 112.1 jit_solution(10652682099227492581)
XLA Ops:
  0.0 5.7 %row_logits.1 = (bf16[24,40,128]{2,1,0:T(8,128)(2,1)}, bf16[192,768]{1,0:T(8,128)(2,1)}) custom-call(bf16[192,768]{1,0:T(8,128)(2,1)} %bitcast.11, s32[1,48]{1,0:T(1,128)} %lens_ref.3, bf16[768,2304]{1,0:T(8,128)(2,1)} %bitcast.19), custom_call_target="tpu_custom_call" | custom-call | tf_op jit(solution)/shard_map/row_logits/pallas_call | solution.py:218
  5.7 33.4 %all_to_all.20.got_ref = bf16[24,40,128]{2,1,0:T(8,128)(2,1)S(1)} all-to-all(bf16[24,40,128]{2,1,0:T(8,128)(2,1)} %get-tuple-element.7), channel_id=1, replica_groups=mesh['section'=32,'depth'=2,'res'=12] {'depth','res'}, dimensions={0} | all-to-all | bytes 491520 | tf_op jit(solution)/shard_map/all_to_all | solution.py:231
  39.2 0.0 copy-start.1
  39.2 0.0 copy-start.2
  39.2 0.0 copy-start.4
  39.2 0.0 copy-start.6
  39.2 0.0 copy-start
  39.2 0.3 sum_shares.1
  39.5 0.0 copy-start.3
  39.5 19.0 %all_to_all.21.tied_ref = bf16[24,40,128]{2,1,0:T(8,128)(2,1)S(1)} all-to-all(bf16[24,40,128]{2,1,0:T(8,128)(2,1)S(1)} %sum_shares.1), channel_id=1, replica_groups=mesh['section'=32,'depth'=2,'res'=12] {'depth','res'}, dimensions={0} | all-to-all | bytes 491520 | tf_op jit(solution)/shard_map/all_to_all | solution.py:231
  58.5 0.0 copy-done.1
  58.5 0.0 copy-done.2
  58.5 0.0 copy-done.4
  58.5 0.0 copy-done.6
  58.5 1.7 %row_mix.1 = bf16[192,768]{1,0:T(8,128)(2,1)S(1)} custom-call(bf16[24,40,128]{2,1,0:T(8,128)(2,1)S(1)} %all_to_all.21.tied_ref, bf16[192,768]{1,0:T(8,128)(2,1)S(1)} %copy-done.4, bf16[192,768]{1,0:T(8,128)(2,1)S(1)} %bitcast.12, s32[1,48]{1,0:T(1,128)S(1)} %copy-done.6, bf16[768,768]{1,0:T(8,128)(2,1)S(1)} %bitcast.16), custom_call_target="tpu_custom_call" | custom-call | tf_op jit(solution)/shard_map/row_mix/pallas_call | solution.py:218
  60.3 0.0 copy-start.5
  60.3 0.0 copy-start.7
  60.3 20.1 %all_to_all.22 = bf16[24,8,768]{2,1,0:T(8,128)(2,1)S(1)} all-to-all(bf16[24,8,768]{2,1,0:T(8,128)(2,1)S(1)} %bitcast.13), channel_id=1, replica_groups=mesh['section'=32,'depth'=2,'res'=12] {'depth','res'}, dimensions={0} | all-to-all | bytes 589824 | tf_op jit(solution)/shard_map/all_to_all | solution.py:231
  80.4 0.0 copy-done
  80.4 0.0 copy-done.3
  80.4 2.3 %column_block.1 = bf16[192,768]{1,0:T(8,128)(2,1)S(1)} custom-call(bf16[192,768]{1,0:T(8,128)(2,1)S(1)} %bitcast.14, s32[1,48]{1,0:T(1,128)S(1)} %copy-done.6, bf16[768,2304]{1,0:T(8,128)(2,1)S(1)} %bitcast.10, bf16[768,768]{1,0:T(8,128)(2,1)S(1)} %bitcast.18), custom_call_target="tpu_custom_call" | custom-call | tf_op jit(solution)/shard_map/column_block/pallas_call | solution.py:218
  82.7 18.3 %all_to_all.23 = bf16[24,8,768]{2,1,0:T(8,128)(2,1)S(1)} all-to-all(bf16[24,8,768]{2,1,0:T(8,128)(2,1)S(1)} %bitcast.15), channel_id=1, replica_groups=mesh['section'=32,'depth'=2,'res'=12] {'depth','res'}, dimensions={0} | all-to-all | bytes 589824 | tf_op jit(solution)/shard_map/all_to_all | solution.py:231
  101.0 0.0 copy-done.5
  101.0 0.0 copy-done.7
  101.0 0.2 finish.1
  101.3 1.9 %collective-permute-start = (bf16[192,768]{1,0:T(8,128)(2,1)S(1)}, bf16[192,768]{1,0:T(8,128)(2,1)S(1)}, u32[]{:S(2)}, u32[]{:S(2)}) collective-permute-start(bf16[192,768]{1,0:T(8,128)(2,1)S(1)} %finish.1), channel_id=1, source_target_pairs={{0,24},{24,48},{48,72},{72,96},{96,120},{120,144},{144,168},{168,1... | collective-permute-start | bytes 884744 | tf_op jit(solution)/shard_map/ppermute | solution.py:300
  103.2 8.2 %collective-permute-done = bf16[192,768]{1,0:T(8,128)(2,1)S(1)} collective-permute-done((bf16[192,768]{1,0:T(8,128)(2,1)S(1)}, bf16[192,768]{1,0:T(8,128)(2,1)S(1)}, u32[]{:S(2)}, u32[]{:S(2)}) %collective-permute-start) | collective-permute-done | bytes 294944 | tf_op jit(solution)/shard_map/ppermute | solution.py:300
  111.4 0.7 copy.10
Async XLA Ops:
  39.2 19.3 %copy-start.1 = (bf16[1,2,96,768]{3,2,1,0:T(8,128)(2,1)S(1)}, bf16[1,2,96,768]{3,2,1,0:T(8,128)(2,1)}, u32[]{:S(2)}) copy-start(bf16[1,2,96,768]{3,2,1,0:T(8,128)(2,1)} %param.8) | copy-start | bytes 884740
  39.2 19.4 %copy-start.2 = (bf16[1,768,768]{2,1,0:T(8,128)(2,1)S(1)}, bf16[1,768,768]{2,1,0:T(8,128)(2,1)}, u32[]{:S(2)}) copy-start(bf16[1,768,768]{2,1,0:T(8,128)(2,1)} %param.13) | copy-start | bytes 3538948
  39.2 19.4 %copy-start.4 = (bf16[192,768]{1,0:T(8,128)(2,1)S(1)}, bf16[192,768]{1,0:T(8,128)(2,1)}, u32[]{:S(2)}) copy-start(bf16[192,768]{1,0:T(8,128)(2,1)} %get-tuple-element.8.v_ref) | copy-start | bytes 884740
  39.2 19.4 %copy-start.6 = (s32[1,48]{1,0:T(1,128)S(1)}, s32[1,48]{1,0:T(1,128)}, u32[]{:S(2)}) copy-start(s32[1,48]{1,0:T(1,128)} %lens_ref.3) | copy-start | bytes 580
  39.2 41.2 %copy-start = (bf16[1,768,2304]{2,1,0:T(8,128)(2,1)S(1)}, bf16[1,768,2304]{2,1,0:T(8,128)(2,1)}, u32[]{:S(2)}) copy-start(bf16[1,768,2304]{2,1,0:T(8,128)(2,1)} %param.14) | copy-start | bytes 10616836
  39.5 40.9 %copy-start.3 = (bf16[1,768,768]{2,1,0:T(8,128)(2,1)S(1)}, bf16[1,768,768]{2,1,0:T(8,128)(2,1)}, u32[]{:S(2)}) copy-start(bf16[1,768,768]{2,1,0:T(8,128)(2,1)} %param.15) | copy-start | bytes 3538948
  60.3 40.8 %copy-start.5 = (bf16[33,768]{1,0:T(8,128)(2,1)S(1)}, bf16[33,768]{1,0:T(8,128)(2,1)}, u32[]{:S(2)}) copy-start(bf16[33,768]{1,0:T(8,128)(2,1)} %embed_ref.1) | copy-start | bytes 152068
  60.3 40.8 %copy-start.7 = (s32[2,96]{1,0:T(2,128)S(1)}, s32[2,96]{1,0:T(2,128)}, u32[]{:S(2)}) copy-start(s32[2,96]{1,0:T(2,128)} %tokens_ref.1) | copy-start | bytes 2308
  101.3 10.2 %collective-permute-start = (bf16[192,768]{1,0:T(8,128)(2,1)S(1)}, bf16[192,768]{1,0:T(8,128)(2,1)S(1)}, u32[]{:S(2)}, u32[]{:S(2)}) collective-permute-start(bf16[192,768]{1,0:T(8,128)(2,1)S(1)} %finish.1), channel_id=1, source_target_pairs={{0,24},{24,48},{48,72},{72,96},{96,120},{120,144},{144,168},{168,1... | collective-permute-start | bytes 884744 | tf_op jit(solution)/shard_map/ppermute | solution.py:300

commit v4 on v3

--- a/solution.py
+++ b/solution.py
@@ -40,6 +40,11 @@
     off = values - center
     spread = jnp.mean(off * off, axis=-1, keepdims=True)
     return (off * lax.rsqrt(spread + 1e-05)).astype(BF16)
+
+
+def turned(place, ring):
+    back = 3 * ring - 1 - place
+    return (place if place < ring else back) if isinstance(place, int) else jnp.where(place < ring, place, back)
 
 
 def place_of():
@@ -172,13 +177,14 @@
     x = x_ref[...]
     packed = dot(normalize(x), wqkv_ref[...]).astype(BF16)
     token = iota((all_rows, n), 1)
-    row_of = token // chunk * rows + token % rows
+    ring = devices // 2
+    row_of = turned(token // chunk, ring) * rows + token % rows
     spread_rows = (row_of == iota((all_rows, n), 0)).astype(BF16)
     lens = jnp.broadcast_to(lens_ref[...].astype(F32), (8, all_rows)).astype(BF16)
     token_lens = dot(lens, spread_rows)[0:1]
     residue_k = iota((n, n), 1) % chunk // rows
     residue_q = iota((n, n), 0) % chunk // rows
-    inside = (place_of() * columns + iota((1, n), 1) % chunk // rows).astype(F32) < token_lens
+    inside = (turned(place_of(), ring) * columns + iota((1, n), 1) % chunk // rows).astype(F32) < token_lens
     bias = jnp.where((residue_k == residue_q) & inside, 0.0, NEG)
     bias = jnp.concatenate([bias, bias], axis=0)
     for pair in range(H // 2):
@@ -228,7 +234,10 @@
 
 
 def exchange(blocks):
-    return lax.all_to_all(blocks, GROUP, split_axis=0, concat_axis=0, tiled=True)
+    order = [turned(i, lax.axis_size("res")) for i in range(blocks.shape[0])]
+    return lax.all_to_all(
+        blocks, GROUP, split_axis=0, concat_axis=0, tiled=True, axis_index_groups=[order]
+    )
 
 
 def local(slab, tokens, lengths, embed, row_qkv, row_out, col_qkv, col_out):

time: 113 us -> 111 us (0.982)
  blocking collectives: 90.8 us -> 89.6 us
    all_to_all x4, blocking collectives: 90.8 us -> 89.6 us  [exchange(): lax.all_to_all(blocks, GROUP, split_axis=0, concat_axis=0, tiled=True, ax...]
where the time goes in v4:
time: 111 us
  blocking collectives  89.6 us (81%)
  Pallas kernels  10.3 us (9%)
  waiting for transfers between devices  8.22 us (7%)
  starting transfers between devices  1.92 us (2%)
    all_to_all x4, blocking collectives, exchange(): lax.all_to_all(blocks, GROUP, split_axis=0, concat_axis=0, tiled=True, ax...  89.6 us
    pallas_call x5, Pallas kernels, call(): pl.pallas_call(body, out_shape=shapes, in_specs=[hbm if i in far else vme...  10.3 us
    ppermute x1, waiting for transfers between devices, local(): lax.ppermute(out, 'section', [(s, (s + 1) % sections) for s in range(sect...  8.22 us
  transfers between devices with their start and end apart: 1, of which 1 were waited for; matrix products, arithmetic and copies ran while one was open for 0% of the time, Pallas kernels for 0%

profile of v4, /device:TPU:32, one launch (start us, length us, event | category | flops | bytes accessed | tf_op | source)
XLA Modules:
  0.0 110.9 jit_solution(6140549245575374480)
XLA Ops:
  0.0 5.7 %row_logits.1 = (bf16[24,40,128]{2,1,0:T(8,128)(2,1)}, bf16[192,768]{1,0:T(8,128)(2,1)}) custom-call(bf16[192,768]{1,0:T(8,128)(2,1)} %bitcast.11, s32[1,48]{1,0:T(1,128)} %lens_ref.3, bf16[768,2304]{1,0:T(8,128)(2,1)} %bitcast.19), custom_call_target="tpu_custom_call" | custom-call | tf_op jit(solution)/shard_map/row_logits/pallas_call | solution.py:224
  5.7 32.3 %all_to_all.20.got_ref = bf16[24,40,128]{2,1,0:T(8,128)(2,1)S(1)} all-to-all(bf16[24,40,128]{2,1,0:T(8,128)(2,1)} %get-tuple-element.7), channel_id=1, replica_groups={{0,1,2,3,4,5,6,7,8,9,10,11,23,22,21,20,19,18,17,16,15,14,13,12},{24,25,..., dimensions={0} | all-to-all | bytes 491520 | tf_op jit(solution)/shard_map/all_to_all | solution.py:238
  38.1 0.0 copy-start.1
  38.1 0.0 copy-start.2
  38.1 0.0 copy-start.4
  38.1 0.0 copy-start.6
  38.1 0.0 copy-start
  38.1 0.3 sum_shares.1
  38.4 0.0 copy-start.3
  38.4 18.6 %all_to_all.21.tied_ref = bf16[24,40,128]{2,1,0:T(8,128)(2,1)S(1)} all-to-all(bf16[24,40,128]{2,1,0:T(8,128)(2,1)S(1)} %sum_shares.1), channel_id=1, replica_groups={{0,1,2,3,4,5,6,7,8,9,10,11,23,22,21,20,19,18,17,16,15,14,13,12},{24,25,..., dimensions={0} | all-to-all | bytes 491520 | tf_op jit(solution)/shard_map/all_to_all | solution.py:238
  57.0 0.0 copy-done.1
  57.0 0.0 copy-done.2
  57.0 0.0 copy-done.4
  57.0 0.0 copy-done.6
  57.1 1.7 %row_mix.1 = bf16[192,768]{1,0:T(8,128)(2,1)S(1)} custom-call(bf16[24,40,128]{2,1,0:T(8,128)(2,1)S(1)} %all_to_all.21.tied_ref, bf16[192,768]{1,0:T(8,128)(2,1)S(1)} %copy-done.4, bf16[192,768]{1,0:T(8,128)(2,1)S(1)} %bitcast.12, s32[1,48]{1,0:T(1,128)S(1)} %copy-done.6, bf16[768,768]{1,0:T(8,128)(2,1)S(1)} %bitcast.16), custom_call_target="tpu_custom_call" | custom-call | tf_op jit(solution)/shard_map/row_mix/pallas_call | solution.py:224
  58.8 0.0 copy-start.5
  58.8 0.0 copy-start.7
  58.8 19.3 %all_to_all.22 = bf16[24,8,768]{2,1,0:T(8,128)(2,1)S(1)} all-to-all(bf16[24,8,768]{2,1,0:T(8,128)(2,1)S(1)} %bitcast.13), channel_id=1, replica_groups={{0,1,2,3,4,5,6,7,8,9,10,11,23,22,21,20,19,18,17,16,15,14,13,12},{24,25,..., dimensions={0} | all-to-all | bytes 589824 | tf_op jit(solution)/shard_map/all_to_all | solution.py:238
  78.1 0.0 copy-done
  78.1 0.0 copy-done.3
  78.1 2.3 %column_block.1 = bf16[192,768]{1,0:T(8,128)(2,1)S(1)} custom-call(bf16[192,768]{1,0:T(8,128)(2,1)S(1)} %bitcast.14, s32[1,48]{1,0:T(1,128)S(1)} %copy-done.6, bf16[768,2304]{1,0:T(8,128)(2,1)S(1)} %bitcast.10, bf16[768,768]{1,0:T(8,128)(2,1)S(1)} %bitcast.18), custom_call_target="tpu_custom_call" | custom-call | tf_op jit(solution)/shard_map/column_block/pallas_call | solution.py:224
  80.4 19.4 %all_to_all.23 = bf16[24,8,768]{2,1,0:T(8,128)(2,1)S(1)} all-to-all(bf16[24,8,768]{2,1,0:T(8,128)(2,1)S(1)} %bitcast.15), channel_id=1, replica_groups={{0,1,2,3,4,5,6,7,8,9,10,11,23,22,21,20,19,18,17,16,15,14,13,12},{24,25,..., dimensions={0} | all-to-all | bytes 589824 | tf_op jit(solution)/shard_map/all_to_all | solution.py:238
  99.8 0.0 copy-done.5
  99.8 0.0 copy-done.7
  99.8 0.2 finish.1
  100.0 1.9 %collective-permute-start = (bf16[192,768]{1,0:T(8,128)(2,1)S(1)}, bf16[192,768]{1,0:T(8,128)(2,1)S(1)}, u32[]{:S(2)}, u32[]{:S(2)}) collective-permute-start(bf16[192,768]{1,0:T(8,128)(2,1)S(1)} %finish.1), channel_id=1, source_target_pairs={{0,24},{24,48},{48,72},{72,96},{96,120},{120,144},{144,168},{168,1... | collective-permute-start | bytes 884744 | tf_op jit(solution)/shard_map/ppermute | solution.py:309
  102.0 8.2 %collective-permute-done = bf16[192,768]{1,0:T(8,128)(2,1)S(1)} collective-permute-done((bf16[192,768]{1,0:T(8,128)(2,1)S(1)}, bf16[192,768]{1,0:T(8,128)(2,1)S(1)}, u32[]{:S(2)}, u32[]{:S(2)}) %collective-permute-start) | collective-permute-done | bytes 294944 | tf_op jit(solution)/shard_map/ppermute | solution.py:309
  110.2 0.7 copy.10
Async XLA Ops:
  38.1 19.0 %copy-start.1 = (bf16[1,2,96,768]{3,2,1,0:T(8,128)(2,1)S(1)}, bf16[1,2,96,768]{3,2,1,0:T(8,128)(2,1)}, u32[]{:S(2)}) copy-start(bf16[1,2,96,768]{3,2,1,0:T(8,128)(2,1)} %param.8) | copy-start | bytes 884740
  38.1 19.0 %copy-start.2 = (bf16[1,768,768]{2,1,0:T(8,128)(2,1)S(1)}, bf16[1,768,768]{2,1,0:T(8,128)(2,1)}, u32[]{:S(2)}) copy-start(bf16[1,768,768]{2,1,0:T(8,128)(2,1)} %param.13) | copy-start | bytes 3538948
  38.1 19.0 %copy-start.4 = (bf16[192,768]{1,0:T(8,128)(2,1)S(1)}, bf16[192,768]{1,0:T(8,128)(2,1)}, u32[]{:S(2)}) copy-start(bf16[192,768]{1,0:T(8,128)(2,1)} %get-tuple-element.8.v_ref) | copy-start | bytes 884740
  38.1 19.0 %copy-start.6 = (s32[1,48]{1,0:T(1,128)S(1)}, s32[1,48]{1,0:T(1,128)}, u32[]{:S(2)}) copy-start(s32[1,48]{1,0:T(1,128)} %lens_ref.3) | copy-start | bytes 580
  38.1 40.0 %copy-start = (bf16[1,768,2304]{2,1,0:T(8,128)(2,1)S(1)}, bf16[1,768,2304]{2,1,0:T(8,128)(2,1)}, u32[]{:S(2)}) copy-start(bf16[1,768,2304]{2,1,0:T(8,128)(2,1)} %param.14) | copy-start | bytes 10616836
  38.4 39.7 %copy-start.3 = (bf16[1,768,768]{2,1,0:T(8,128)(2,1)S(1)}, bf16[1,768,768]{2,1,0:T(8,128)(2,1)}, u32[]{:S(2)}) copy-start(bf16[1,768,768]{2,1,0:T(8,128)(2,1)} %param.15) | copy-start | bytes 3538948
  58.8 41.0 %copy-start.5 = (bf16[33,768]{1,0:T(8,128)(2,1)S(1)}, bf16[33,768]{1,0:T(8,128)(2,1)}, u32[]{:S(2)}) copy-start(bf16[33,768]{1,0:T(8,128)(2,1)} %embed_ref.1) | copy-start | bytes 152068
  58.8 41.0 %copy-start.7 = (s32[2,96]{1,0:T(2,128)S(1)}, s32[2,96]{1,0:T(2,128)}, u32[]{:S(2)}) copy-start(s32[2,96]{1,0:T(2,128)} %tokens_ref.1) | copy-start | bytes 2308
  100.0 10.2 %collective-permute-start = (bf16[192,768]{1,0:T(8,128)(2,1)S(1)}, bf16[192,768]{1,0:T(8,128)(2,1)S(1)}, u32[]{:S(2)}, u32[]{:S(2)}) collective-permute-start(bf16[192,768]{1,0:T(8,128)(2,1)S(1)} %finish.1), channel_id=1, source_target_pairs={{0,24},{24,48},{48,72},{72,96},{96,120},{120,144},{144,168},{168,1... | collective-permute-start | bytes 884744 | tf_op jit(solution)/shard_map/ppermute | solution.py:309
